TPU v7x, 32 devices: a whole 2x2x4 slice. The times are simulated.
32 devices in a mesh: dp: 16 (over z, y, x), fsdp: 2 (over core).
Axes of the slice: x: 2, y: 2, z: 4, core: 2. Of those that a mesh axis runs over, the one named last changes fastest.
Arguments:
- hidden_in: bfloat16 [32, 704, 1024], P(('dp', 'fsdp')), may hold values from -6 to 6
- cluster_lengths: int32 [32, 8], P(('dp', 'fsdp')), may hold values from 1 to 192, 704 in all within a row
- norm_gain: bfloat16 [1024], P('fsdp'), may hold values from 0.099609375 to 1.8984375
- in_proj: bfloat16 [1024, 4096], P('fsdp'), may hold values from -0.1875 to 0.1875
- conv_weight: bfloat16 [4, 2048], P(None, 'fsdp'), may hold values from -3 to 3
- conv_bias: bfloat16 [2048], P('fsdp'), may hold values from -3 to 3
- x_proj: bfloat16 [2048, 96], P('fsdp'), may hold values from -0.125 to 0.125
- dt_proj: bfloat16 [64, 2048], P(None, 'fsdp'), may hold values from -0.75 to 0.75
- dt_bias: bfloat16 [2048], P('fsdp'), may hold values from -6 to -2.5
- a_log: bfloat16 [16, 2048], P(None, 'fsdp'), may hold values from 0 to 2.765625
- skip_gain: bfloat16 [2048], P('fsdp'), may hold values from 0.5 to 1.5
- out_proj: bfloat16 [2048, 1024], P('fsdp'), may hold values from -0.125 to 0.125
- out_grad: bfloat16 [32, 704, 1024], P(('dp', 'fsdp')), may hold values from -6 to 6
Outputs:
- layer_out: bfloat16 [32, 704, 1024], P(('dp', 'fsdp'))
- input_grad: float32 [32, 704, 1024], P(('dp', 'fsdp'))
- grad_norm_gain: float32 [1024], P('fsdp')
- grad_in_proj: float32 [1024, 4096], P('fsdp')
- grad_conv_weight: float32 [4, 2048], P(None, 'fsdp')
- grad_conv_bias: float32 [2048], P('fsdp')
- grad_x_proj: float32 [2048, 96], P('fsdp')
- grad_dt_proj: float32 [64, 2048], P(None, 'fsdp')
- grad_dt_bias: float32 [2048], P('fsdp')
- grad_a_log: float32 [16, 2048], P(None, 'fsdp')
- grad_skip_gain: float32 [2048], P('fsdp')
- grad_out_proj: float32 [2048, 1024], P('fsdp')
Inputs may be any that keep to these rules, and one draw needn't show every extreme that they name: `cluster_lengths`: each row lists the 8 cluster lengths of one context; they sum to 704, and each context's longest cluster has exactly 192 tokens.
All inputs are finite; a program needn't handle non-finite values.
Results may differ from a plain program's by a relative error of at most 0.011.
Values may be sent and summed in bfloat16 or wider, within the bound.
A program may use at most 256 MiB of HBM per device.

v0:
```python
import jax
import jax.numpy as jnp
from jax import lax
from jax.sharding import PartitionSpec as P

SPAN = 64


norm_eps = 1e-05


def cluster_offsets(lengths, total_len):
    end_points = jnp.cumsum(lengths, axis=1, dtype=jnp.int32)
    start_points = end_points - lengths
    where_at = jnp.arange(total_len, dtype=jnp.int32)
    inside = (where_at[None, None, :] >= start_points[:, :, None]) & (
        where_at[None, None, :] < end_points[:, :, None]
    )
    first_spot = jnp.sum(jnp.where(inside, start_points[:, :, None], 0), axis=1, dtype=jnp.int32)
    return where_at[None, :] - first_spot


def rms_piece(inputs, gain_vec):
    mean_sq = jnp.mean(inputs * inputs, axis=-1, keepdims=True)
    return inputs * lax.rsqrt(mean_sq + norm_eps) * gain_vec


def conv_piece(upper_part, conv_taps, conv_shift, offsets):
    tap_count = conv_taps.shape[0]
    total_len = upper_part.shape[1]
    summed = conv_shift + conv_taps[tap_count - 1] * upper_part
    for lag_steps in range(1, tap_count):
        shifted = jnp.pad(upper_part, ((0, 0), (lag_steps, 0), (0, 0)))[:, :total_len]
        summed = summed + conv_taps[tap_count - 1 - lag_steps] * jnp.where(
            (offsets >= lag_steps)[..., None], shifted, 0.0
        )
    return summed * jax.nn.sigmoid(summed)


def gate_piece(y_full, gate_z):
    return y_full * gate_z * jax.nn.sigmoid(gate_z)


def span_run(state_now, part_dt, part_b, part_c, part_u, part_keep, decay_rate):

    def token_step(carried, item_now):
        step_dt, step_b, step_c, step_u, step_keep = item_now
        carried = (
            jnp.exp(step_dt[:, None, :] * decay_rate) * step_keep[:, None, None] * carried
            + (step_dt * step_u)[:, None, :] * step_b[:, :, None]
        )
        return (carried, jnp.sum(step_c[:, :, None] * carried, axis=1))

    items = (
        jnp.moveaxis(part_dt, 1, 0),
        jnp.moveaxis(part_b, 1, 0),
        jnp.moveaxis(part_c, 1, 0),
        jnp.moveaxis(part_u, 1, 0),
        jnp.moveaxis(part_keep, 1, 0),
    )
    last_state, outputs = lax.scan(token_step, state_now, items, unroll=8)
    return (jnp.moveaxis(outputs, 0, 1), last_state)


def scan_forward(delta_t, b_in, c_out, inner_act, keep_mask, decay_rate):
    blocks = delta_t.shape[1] // SPAN

    def fore_step(carried, block_idx):
        state_now, outputs = carried
        begin_at = block_idx * SPAN

        def take_block(array_in):
            return lax.dynamic_slice_in_dim(array_in, begin_at, SPAN, 1)

        part_y, state_next = span_run(
            state_now,
            take_block(delta_t),
            take_block(b_in),
            take_block(c_out),
            take_block(inner_act),
            take_block(keep_mask),
            decay_rate,
        )
        return (
            (state_next, lax.dynamic_update_slice_in_dim(outputs, part_y, begin_at, 1)),
            state_now,
        )

    zero_state = jnp.zeros((delta_t.shape[0], decay_rate.shape[0], delta_t.shape[2]), jnp.float32)
    (_, outputs), boundary = lax.scan(
        fore_step, (zero_state, jnp.zeros_like(delta_t)), jnp.arange(blocks)
    )
    return (outputs, boundary)


def scan_backward(d_scan_y, boundary, delta_t, b_in, c_out, inner_act, keep_mask, decay_rate):
    blocks = delta_t.shape[1] // SPAN

    def back_step(carried, block_idx):
        d_state, d_rate, d_delta, d_bin, d_cout, d_inner = carried
        begin_at = block_idx * SPAN

        def take_block(array_in):
            return lax.dynamic_slice_in_dim(array_in, begin_at, SPAN, 1)

        keep_part = take_block(keep_mask)

        def span_local(state_now, part_dt, part_b, part_c, part_u, rate_in):
            return span_run(state_now, part_dt, part_b, part_c, part_u, keep_part, rate_in)

        _, pull_back = jax.vjp(
            span_local,
            boundary[block_idx],
            take_block(delta_t),
            take_block(b_in),
            take_block(c_out),
            take_block(inner_act),
            decay_rate,
        )
        g_state, g_dt, g_b, g_c, g_u, g_rate = pull_back((take_block(d_scan_y), d_state))

        def place_block(buffer, part_new):
            return lax.dynamic_update_slice_in_dim(buffer, part_new, begin_at, 1)

        return (
            (
                g_state,
                d_rate + g_rate,
                place_block(d_delta, g_dt),
                place_block(d_bin, g_b),
                place_block(d_cout, g_c),
                place_block(d_inner, g_u),
            ),
            None,
        )

    start_carry = (
        jnp.zeros_like(boundary[0]),
        jnp.zeros_like(decay_rate),
        jnp.zeros_like(delta_t),
        jnp.zeros_like(b_in),
        jnp.zeros_like(c_out),
        jnp.zeros_like(inner_act),
    )
    finished, _ = lax.scan(back_step, start_carry, jnp.arange(blocks), reverse=True)
    return (finished[2], finished[3], finished[4], finished[5], finished[1])


def shards(
    hidden_in,
    cluster_lengths,
    norm_gain,
    in_proj,
    conv_weight,
    conv_bias,
    x_proj,
    dt_proj,
    dt_bias,
    a_log,
    skip_gain,
    out_proj,
    out_grad,
):
    gathered = (
        lax.all_gather(norm_gain, "fsdp", axis=0, tiled=True),
        lax.all_gather(in_proj, "fsdp", axis=0, tiled=True),
        lax.all_gather(conv_weight, "fsdp", axis=1, tiled=True),
        lax.all_gather(conv_bias, "fsdp", axis=0, tiled=True),
        lax.all_gather(x_proj, "fsdp", axis=0, tiled=True),
        lax.all_gather(dt_proj, "fsdp", axis=1, tiled=True),
        lax.all_gather(dt_bias, "fsdp", axis=0, tiled=True),
        lax.all_gather(a_log, "fsdp", axis=1, tiled=True),
        lax.all_gather(skip_gain, "fsdp", axis=0, tiled=True),
        lax.all_gather(out_proj, "fsdp", axis=0, tiled=True),
    )
    w_gain, w_in, w_conv, b_conv, w_x, w_dt, b_dt, w_alog, w_skip, w_out = gathered
    contexts_here, total_len, model_dim = hidden_in.shape
    inner_dim = w_conv.shape[1]
    rank_dim = w_dt.shape[0]
    state_dim = w_alog.shape[0]
    row_count = contexts_here * total_len
    offsets = cluster_offsets(cluster_lengths, total_len)
    keep_mask = jnp.where(offsets > 0, 1.0, 0.0).astype(jnp.float32)
    inputs = hidden_in.astype(jnp.float32)
    gain_full = w_gain.astype(jnp.float32)
    normed16 = rms_piece(inputs, gain_full).astype(jnp.bfloat16).reshape(row_count, model_dim)
    both = jnp.dot(normed16, w_in, preferred_element_type=jnp.float32).reshape(
        contexts_here, total_len, 2 * inner_dim
    )
    upper_part = both[..., :inner_dim]
    gate_z = both[..., inner_dim:]
    conv_taps = w_conv.astype(jnp.float32)
    conv_shift = b_conv.astype(jnp.float32)
    inner_act = conv_piece(upper_part, conv_taps, conv_shift, offsets)
    inner16 = inner_act.astype(jnp.bfloat16).reshape(row_count, inner_dim)
    projected = jnp.dot(inner16, w_x, preferred_element_type=jnp.float32).reshape(
        contexts_here, total_len, -1
    )
    rank16 = projected[..., :rank_dim].astype(jnp.bfloat16).reshape(row_count, rank_dim)
    b_in = projected[..., rank_dim : rank_dim + state_dim]
    c_out = projected[..., rank_dim + state_dim :]
    dt_pre = jnp.dot(rank16, w_dt, preferred_element_type=jnp.float32).reshape(
        contexts_here, total_len, inner_dim
    ) + b_dt.astype(jnp.float32)
    delta_t = jax.nn.softplus(dt_pre)
    decay_rate = -jnp.exp(w_alog.astype(jnp.float32))
    skip_full = w_skip.astype(jnp.float32)
    scan_y, boundary = scan_forward(delta_t, b_in, c_out, inner_act, keep_mask, decay_rate)
    y_full = scan_y + skip_full * inner_act
    gated16 = gate_piece(y_full, gate_z).astype(jnp.bfloat16).reshape(row_count, inner_dim)
    layer_out = (
        inputs
        + jnp.dot(gated16, w_out, preferred_element_type=jnp.float32).reshape(
            contexts_here, total_len, model_dim
        )
    ).astype(jnp.bfloat16)
    regathered = (
        lax.all_gather(norm_gain, "fsdp", axis=0, tiled=True),
        lax.all_gather(in_proj, "fsdp", axis=0, tiled=True),
        lax.all_gather(conv_weight, "fsdp", axis=1, tiled=True),
        lax.all_gather(conv_bias, "fsdp", axis=0, tiled=True),
        lax.all_gather(x_proj, "fsdp", axis=0, tiled=True),
        lax.all_gather(dt_proj, "fsdp", axis=1, tiled=True),
        lax.all_gather(dt_bias, "fsdp", axis=0, tiled=True),
        lax.all_gather(a_log, "fsdp", axis=1, tiled=True),
        lax.all_gather(skip_gain, "fsdp", axis=0, tiled=True),
        lax.all_gather(out_proj, "fsdp", axis=0, tiled=True),
    )
    w_gain, w_in, w_conv, b_conv, w_x, w_dt, b_dt, w_alog, w_skip, w_out = regathered
    grad_rows = out_grad.reshape(row_count, model_dim)
    g_w_out = jnp.dot(gated16.T, grad_rows, preferred_element_type=jnp.float32)
    d_gated = jnp.dot(grad_rows, w_out.T, preferred_element_type=jnp.float32).reshape(
        contexts_here, total_len, inner_dim
    )
    _, gate_pull = jax.vjp(gate_piece, y_full, gate_z)
    d_y, d_gate_z = gate_pull(d_gated)
    g_skip = jnp.sum(d_y * inner_act, axis=(0, 1))
    d_delta, d_bin, d_cout, d_inner_scan, g_rate = scan_backward(
        d_y, boundary, delta_t, b_in, c_out, inner_act, keep_mask, decay_rate
    )
    g_alog = g_rate * decay_rate
    dt16 = (d_delta * jax.nn.sigmoid(dt_pre)).astype(jnp.bfloat16).reshape(row_count, inner_dim)
    g_b_dt = jnp.sum(dt16.astype(jnp.float32), axis=0)
    g_w_dt = jnp.dot(rank16.T, dt16, preferred_element_type=jnp.float32)
    d_rank = jnp.dot(dt16, w_dt.T, preferred_element_type=jnp.float32).reshape(
        contexts_here, total_len, rank_dim
    )
    proj16 = (
        jnp.concatenate([d_rank, d_bin, d_cout], axis=-1)
        .astype(jnp.bfloat16)
        .reshape(row_count, -1)
    )
    g_w_x = jnp.dot(inner16.T, proj16, preferred_element_type=jnp.float32)
    d_inner = (
        jnp.dot(proj16, w_x.T, preferred_element_type=jnp.float32).reshape(
            contexts_here, total_len, inner_dim
        )
        + d_inner_scan
        + d_y * w_skip.astype(jnp.float32)
    )
    _, conv_pull = jax.vjp(
        lambda part_u, taps_in, shift_in: conv_piece(part_u, taps_in, shift_in, offsets),
        upper_part,
        w_conv.astype(jnp.float32),
        b_conv.astype(jnp.float32),
    )
    d_upper, g_conv, g_b_conv = conv_pull(d_inner)
    both16 = (
        jnp.concatenate([d_upper, d_gate_z], axis=-1)
        .astype(jnp.bfloat16)
        .reshape(row_count, 2 * inner_dim)
    )
    g_w_in = jnp.dot(normed16.T, both16, preferred_element_type=jnp.float32)
    d_normed = jnp.dot(both16, w_in.T, preferred_element_type=jnp.float32).reshape(
        contexts_here, total_len, model_dim
    )
    _, norm_pull = jax.vjp(rms_piece, inputs, w_gain.astype(jnp.float32))
    d_inputs, g_gain = norm_pull(d_normed)
    input_grad = out_grad.astype(jnp.float32) + d_inputs
    grad_share = (
        lax.psum_scatter(g_gain, "fsdp", scatter_dimension=0, tiled=True),
        lax.psum_scatter(g_w_in, "fsdp", scatter_dimension=0, tiled=True),
        lax.psum_scatter(g_conv, "fsdp", scatter_dimension=1, tiled=True),
        lax.psum_scatter(g_b_conv, "fsdp", scatter_dimension=0, tiled=True),
        lax.psum_scatter(g_w_x, "fsdp", scatter_dimension=0, tiled=True),
        lax.psum_scatter(g_w_dt, "fsdp", scatter_dimension=1, tiled=True),
        lax.psum_scatter(g_b_dt, "fsdp", scatter_dimension=0, tiled=True),
        lax.psum_scatter(g_alog, "fsdp", scatter_dimension=1, tiled=True),
        lax.psum_scatter(g_skip, "fsdp", scatter_dimension=0, tiled=True),
        lax.psum_scatter(g_w_out, "fsdp", scatter_dimension=0, tiled=True),
    )
    totals_all = lax.psum(
        (
            grad_share[0],
            grad_share[1],
            grad_share[2],
            grad_share[3],
            grad_share[4],
            grad_share[5],
            grad_share[6],
            grad_share[7],
            grad_share[8],
            grad_share[9],
        ),
        "dp",
    )
    return (
        layer_out,
        input_grad,
        totals_all[0],
        totals_all[1],
        totals_all[2],
        totals_all[3],
        totals_all[4],
        totals_all[5],
        totals_all[6],
        totals_all[7],
        totals_all[8],
        totals_all[9],
    )


def solution(mesh):
    placed = (
        P(("dp", "fsdp"), None, None),
        P(("dp", "fsdp"), None),
        P("fsdp"),
        P("fsdp", None),
        P(None, "fsdp"),
        P("fsdp"),
        P("fsdp", None),
        P(None, "fsdp"),
        P("fsdp"),
        P(None, "fsdp"),
        P("fsdp"),
        P("fsdp", None),
        P(("dp", "fsdp"), None, None),
    )
    return jax.shard_map(
        shards,
        mesh=mesh,
        in_specs=placed,
        out_specs=(
            P(("dp", "fsdp"), None, None),
            P(("dp", "fsdp"), None, None),
            P("fsdp"),
            P("fsdp", None),
            P(None, "fsdp"),
            P("fsdp"),
            P("fsdp", None),
            P(None, "fsdp"),
            P("fsdp"),
            P(None, "fsdp"),
            P("fsdp"),
            P("fsdp", None),
        ),
        check_vma=False,
    )
```

profile of v0, /device:TPU:0, one launch (start us, length us, event | category | flops | bytes accessed | tf_op | source)
XLA Modules:
  0.0 5136.9 jit_solution(6851231482575993029)
XLA Ops:
  102.8 849.5 %while.173 = (s32[]{:T(128)}, f32[1,16,2048]{2,1,0:T(8,128)S(1)}, f32[1,704,2048]{2,1,0:T(8,128)}, f32[11,1,16,2048]{3,2,1,0:T(8,128)}, s32[11]{0:T(128)S(1)}, /...) while((s32[]{:T(128)}, f32[1,16,2048]{2,1,0:T(8,128)S(1)}, ...), condition=%wide.region_14.15_spmd, body=%wide.region_3.14_spmd.sunk | while | flops 2490383 | bytes 6772392 | solution.py:90
  958.9 3650.9 %while.176 = (s32[]{:T(128)}, f32[1,16,2048]{2,1,0:T(8,128)S(1)}, f32[16,2048]{1,0:T(8,128)S(1)}, f32[1,704,2048]{2,1,0:T(8,128)}, bf16[1,704,16]{1,2,0:T(8,128)...) while((s32[]{:T(128)}, f32[1,16,2048]{2,1,0:T(8,128)S(1)}, ...), condition=%wide.region_52.53_spmd.clone, body=%wide.region_15.52_spmd.clone.sunk | while | flops 6897433 | bytes 36574564 | solution.py:145
  967.0 147.4 %while.178 = (s32[]{:T(128)}, f32[1,16,2048]{2,1,0:T(8,128)S(1)}, f32[8,8,1,1,2048]{4,3,2,1,0:T(1,128)}, f32[8,8,1,16,2048]{4,3,1,2,0:T(8,128)}, f32[8,8,1,1,1]{...) while((s32[]{:T(128)}, f32[1,16,2048]{2,1,0:T(8,128)S(1)}, ...), condition=%wide.region_17.17_spmd, body=%wide.region_16.16_spmd.sunk | while | flops 2523141 | bytes 16960852 | solution.py:61
  1118.4 169.5 %while.179 = (s32[]{:T(128)}, f32[16,2048]{1,0:T(8,128)S(1)}, f32[1,16,2048]{2,1,0:T(8,128)S(1)}, f32[8,8,1,2048]{3,2,1,0:T(1,128)S(1)}, bf16[8,8,1,16]{3,1,2,0:...) while((s32[]{:T(128)}, f32[16,2048]{1,0:T(8,128)S(1)}, ...), condition=%wide.region_51.51_spmd.clone, body=%wide.region_18.50_spmd.clone.sunk | while | flops 4308745 | bytes 11579443 | solution.py:61
  1298.8 147.4 %while.178 = (s32[]{:T(128)}, f32[1,16,2048]{2,1,0:T(8,128)S(1)}, f32[8,8,1,1,2048]{4,3,2,1,0:T(1,128)}, f32[8,8,1,16,2048]{4,3,1,2,0:T(8,128)}, f32[8,8,1,1,1]{...) while((s32[]{:T(128)}, f32[1,16,2048]{2,1,0:T(8,128)S(1)}, ...), condition=%wide.region_17.17_spmd, body=%wide.region_16.16_spmd.sunk | while | flops 2523141 | bytes 16960852 | solution.py:61
  1450.2 169.5 %while.179 = (s32[]{:T(128)}, f32[16,2048]{1,0:T(8,128)S(1)}, f32[1,16,2048]{2,1,0:T(8,128)S(1)}, f32[8,8,1,2048]{3,2,1,0:T(1,128)S(1)}, bf16[8,8,1,16]{3,1,2,0:...) while((s32[]{:T(128)}, f32[16,2048]{1,0:T(8,128)S(1)}, ...), condition=%wide.region_51.51_spmd.clone, body=%wide.region_18.50_spmd.clone.sunk | while | flops 4308745 | bytes 11579443 | solution.py:61
  1630.8 147.4 %while.178 = (s32[]{:T(128)}, f32[1,16,2048]{2,1,0:T(8,128)S(1)}, f32[8,8,1,1,2048]{4,3,2,1,0:T(1,128)}, f32[8,8,1,16,2048]{4,3,1,2,0:T(8,128)}, f32[8,8,1,1,1]{...) while((s32[]{:T(128)}, f32[1,16,2048]{2,1,0:T(8,128)S(1)}, ...), condition=%wide.region_17.17_spmd, body=%wide.region_16.16_spmd.sunk | while | flops 2523141 | bytes 16960852 | solution.py:61
  1782.2 169.5 %while.179 = (s32[]{:T(128)}, f32[16,2048]{1,0:T(8,128)S(1)}, f32[1,16,2048]{2,1,0:T(8,128)S(1)}, f32[8,8,1,2048]{3,2,1,0:T(1,128)S(1)}, bf16[8,8,1,16]{3,1,2,0:...) while((s32[]{:T(128)}, f32[16,2048]{1,0:T(8,128)S(1)}, ...), condition=%wide.region_51.51_spmd.clone, body=%wide.region_18.50_spmd.clone.sunk | while | flops 4308745 | bytes 11579443 | solution.py:61
  1962.7 147.4 %while.178 = (s32[]{:T(128)}, f32[1,16,2048]{2,1,0:T(8,128)S(1)}, f32[8,8,1,1,2048]{4,3,2,1,0:T(1,128)}, f32[8,8,1,16,2048]{4,3,1,2,0:T(8,128)}, f32[8,8,1,1,1]{...) while((s32[]{:T(128)}, f32[1,16,2048]{2,1,0:T(8,128)S(1)}, ...), condition=%wide.region_17.17_spmd, body=%wide.region_16.16_spmd.sunk | while | flops 2523141 | bytes 16960852 | solution.py:61
  2114.0 169.5 %while.179 = (s32[]{:T(128)}, f32[16,2048]{1,0:T(8,128)S(1)}, f32[1,16,2048]{2,1,0:T(8,128)S(1)}, f32[8,8,1,2048]{3,2,1,0:T(1,128)S(1)}, bf16[8,8,1,16]{3,1,2,0:...) while((s32[]{:T(128)}, f32[16,2048]{1,0:T(8,128)S(1)}, ...), condition=%wide.region_51.51_spmd.clone, body=%wide.region_18.50_spmd.clone.sunk | while | flops 4308745 | bytes 11579443 | solution.py:61
  2294.7 147.4 %while.178 = (s32[]{:T(128)}, f32[1,16,2048]{2,1,0:T(8,128)S(1)}, f32[8,8,1,1,2048]{4,3,2,1,0:T(1,128)}, f32[8,8,1,16,2048]{4,3,1,2,0:T(8,128)}, f32[8,8,1,1,1]{...) while((s32[]{:T(128)}, f32[1,16,2048]{2,1,0:T(8,128)S(1)}, ...), condition=%wide.region_17.17_spmd, body=%wide.region_16.16_spmd.sunk | while | flops 2523141 | bytes 16960852 | solution.py:61
  2446.0 169.5 %while.179 = (s32[]{:T(128)}, f32[16,2048]{1,0:T(8,128)S(1)}, f32[1,16,2048]{2,1,0:T(8,128)S(1)}, f32[8,8,1,2048]{3,2,1,0:T(1,128)S(1)}, bf16[8,8,1,16]{3,1,2,0:...) while((s32[]{:T(128)}, f32[16,2048]{1,0:T(8,128)S(1)}, ...), condition=%wide.region_51.51_spmd.clone, body=%wide.region_18.50_spmd.clone.sunk | while | flops 4308745 | bytes 11579443 | solution.py:61
  2626.5 147.4 %while.178 = (s32[]{:T(128)}, f32[1,16,2048]{2,1,0:T(8,128)S(1)}, f32[8,8,1,1,2048]{4,3,2,1,0:T(1,128)}, f32[8,8,1,16,2048]{4,3,1,2,0:T(8,128)}, f32[8,8,1,1,1]{...) while((s32[]{:T(128)}, f32[1,16,2048]{2,1,0:T(8,128)S(1)}, ...), condition=%wide.region_17.17_spmd, body=%wide.region_16.16_spmd.sunk | while | flops 2523141 | bytes 16960852 | solution.py:61
  2777.8 169.5 %while.179 = (s32[]{:T(128)}, f32[16,2048]{1,0:T(8,128)S(1)}, f32[1,16,2048]{2,1,0:T(8,128)S(1)}, f32[8,8,1,2048]{3,2,1,0:T(1,128)S(1)}, bf16[8,8,1,16]{3,1,2,0:...) while((s32[]{:T(128)}, f32[16,2048]{1,0:T(8,128)S(1)}, ...), condition=%wide.region_51.51_spmd.clone, body=%wide.region_18.50_spmd.clone.sunk | while | flops 4308745 | bytes 11579443 | solution.py:61
  2958.5 147.4 %while.178 = (s32[]{:T(128)}, f32[1,16,2048]{2,1,0:T(8,128)S(1)}, f32[8,8,1,1,2048]{4,3,2,1,0:T(1,128)}, f32[8,8,1,16,2048]{4,3,1,2,0:T(8,128)}, f32[8,8,1,1,1]{...) while((s32[]{:T(128)}, f32[1,16,2048]{2,1,0:T(8,128)S(1)}, ...), condition=%wide.region_17.17_spmd, body=%wide.region_16.16_spmd.sunk | while | flops 2523141 | bytes 16960852 | solution.py:61
  3109.8 169.5 %while.179 = (s32[]{:T(128)}, f32[16,2048]{1,0:T(8,128)S(1)}, f32[1,16,2048]{2,1,0:T(8,128)S(1)}, f32[8,8,1,2048]{3,2,1,0:T(1,128)S(1)}, bf16[8,8,1,16]{3,1,2,0:...) while((s32[]{:T(128)}, f32[16,2048]{1,0:T(8,128)S(1)}, ...), condition=%wide.region_51.51_spmd.clone, body=%wide.region_18.50_spmd.clone.sunk | while | flops 4308745 | bytes 11579443 | solution.py:61
  3290.3 147.4 %while.178 = (s32[]{:T(128)}, f32[1,16,2048]{2,1,0:T(8,128)S(1)}, f32[8,8,1,1,2048]{4,3,2,1,0:T(1,128)}, f32[8,8,1,16,2048]{4,3,1,2,0:T(8,128)}, f32[8,8,1,1,1]{...) while((s32[]{:T(128)}, f32[1,16,2048]{2,1,0:T(8,128)S(1)}, ...), condition=%wide.region_17.17_spmd, body=%wide.region_16.16_spmd.sunk | while | flops 2523141 | bytes 16960852 | solution.py:61
  3441.7 169.5 %while.179 = (s32[]{:T(128)}, f32[16,2048]{1,0:T(8,128)S(1)}, f32[1,16,2048]{2,1,0:T(8,128)S(1)}, f32[8,8,1,2048]{3,2,1,0:T(1,128)S(1)}, bf16[8,8,1,16]{3,1,2,0:...) while((s32[]{:T(128)}, f32[16,2048]{1,0:T(8,128)S(1)}, ...), condition=%wide.region_51.51_spmd.clone, body=%wide.region_18.50_spmd.clone.sunk | while | flops 4308745 | bytes 11579443 | solution.py:61
  3773.7 169.5 %while.179 = (s32[]{:T(128)}, f32[16,2048]{1,0:T(8,128)S(1)}, f32[1,16,2048]{2,1,0:T(8,128)S(1)}, f32[8,8,1,2048]{3,2,1,0:T(1,128)S(1)}, bf16[8,8,1,16]{3,1,2,0:...) while((s32[]{:T(128)}, f32[16,2048]{1,0:T(8,128)S(1)}, ...), condition=%wide.region_51.51_spmd.clone, body=%wide.region_18.50_spmd.clone.sunk | while | flops 4308745 | bytes 11579443 | solution.py:61
  3954.2 147.4 %while.178 = (s32[]{:T(128)}, f32[1,16,2048]{2,1,0:T(8,128)S(1)}, f32[8,8,1,1,2048]{4,3,2,1,0:T(1,128)}, f32[8,8,1,16,2048]{4,3,1,2,0:T(8,128)}, f32[8,8,1,1,1]{...) while((s32[]{:T(128)}, f32[1,16,2048]{2,1,0:T(8,128)S(1)}, ...), condition=%wide.region_17.17_spmd, body=%wide.region_16.16_spmd.sunk | while | flops 2523141 | bytes 16960852 | solution.py:61
  4105.5 169.5 %while.179 = (s32[]{:T(128)}, f32[16,2048]{1,0:T(8,128)S(1)}, f32[1,16,2048]{2,1,0:T(8,128)S(1)}, f32[8,8,1,2048]{3,2,1,0:T(1,128)S(1)}, bf16[8,8,1,16]{3,1,2,0:...) while((s32[]{:T(128)}, f32[16,2048]{1,0:T(8,128)S(1)}, ...), condition=%wide.region_51.51_spmd.clone, body=%wide.region_18.50_spmd.clone.sunk | while | flops 4308745 | bytes 11579443 | solution.py:61
  4286.1 147.4 %while.178 = (s32[]{:T(128)}, f32[1,16,2048]{2,1,0:T(8,128)S(1)}, f32[8,8,1,1,2048]{4,3,2,1,0:T(1,128)}, f32[8,8,1,16,2048]{4,3,1,2,0:T(8,128)}, f32[8,8,1,1,1]{...) while((s32[]{:T(128)}, f32[1,16,2048]{2,1,0:T(8,128)S(1)}, ...), condition=%wide.region_17.17_spmd, body=%wide.region_16.16_spmd.sunk | while | flops 2523141 | bytes 16960852 | solution.py:61
  4437.5 169.5 %while.179 = (s32[]{:T(128)}, f32[16,2048]{1,0:T(8,128)S(1)}, f32[1,16,2048]{2,1,0:T(8,128)S(1)}, f32[8,8,1,2048]{3,2,1,0:T(1,128)S(1)}, bf16[8,8,1,16]{3,1,2,0:...) while((s32[]{:T(128)}, f32[16,2048]{1,0:T(8,128)S(1)}, ...), condition=%wide.region_51.51_spmd.clone, body=%wide.region_18.50_spmd.clone.sunk | while | flops 4308745 | bytes 11579443 | solution.py:61
  4825.2 292.9 %all-reduce.19.cloned.1.call-done = (f32[512,4096]{1,0:T(8,128)}, f32[1024,96]{0,1:T(8,128)}, f32[64,1024]{1,0:T(8,128)}, f32[16,1024]{1,0:T(8,128)}, f32[1024,1024]{1,0:T(8,128)}) async-done(((f32[512,4096]{1,0:T(8,128)}, f32[1024,96]{0,1:T(8,128)}, f32[64,1024]{1,0:T(8,128)}, f32[16,1024]{1,0:T(8,128)}, f32[1024,1024]{1,0:T(8,128)}), (f32[512,4096]{1,0:T(8,128)}, f32[1024,96]{0,1:T(8,128)}, ...) | async-done | bytes 13303824 | tf_op jit(solution)/shard_map/psum | solution.py:292
  (12206 shorter events, 5683.0 us)
Async XLA Ops:
  7.3 25.0 all-gather.4.cloned.1.call-start
  8.0 41.4 all-gather.6.cloned.1.call-start
  8.8 4680.7 %reduce-scatter.15.cloned.1.call-start = ((), (), s32[]{:S(2)}) async-start(), calls=%async_computation.11 | async-start | bytes 196608 | tf_op jit(solution)/shard_map/reduce_scatter | solution.py:288
  10.8 30.2 copy-start.20
  14.6 71.0 %copy-start.32 = (f32[2048]{0:T(1024)}, f32[2048]{0:T(1024)S(1)}, u32[]{:S(2)}) copy-start(f32[2048]{0:T(1024)S(1)} %convert_element_type.73) | copy-start | bytes 24580
  18.2 22.7 copy-start.17
  20.2 63.8 %copy-start.12 = (bf16[64,2048]{1,0:T(8,128)(2,1)}, bf16[64,2048]{1,0:T(8,128)(2,1)S(1)}, u32[]{:S(2)}) copy-start(bf16[64,2048]{1,0:T(8,128)(2,1)S(1)} %all_gather.43) | copy-start | bytes 786436
  22.9 18.1 copy-start.35
  22.9 26.5 copy-start.48
  22.9 26.5 copy-start.50
  22.9 26.5 copy-start.52
  23.0 26.4 copy-start.37
  23.0 26.4 copy-start.39
  23.0 26.4 copy-start.41
  23.0 26.4 copy-start.43
  958.9 3650.9 %copy-start.33 = (f32[2048]{0:T(1024)S(1)}, f32[2048]{0:T(1024)}, u32[]{:S(2)}) copy-start(f32[2048]{0:T(1024)} %copy-done.32) | copy-start | bytes 24580
  4615.8 73.6 %reduce-scatter.13.cloned.1.call-start = ((), (), s32[]{:S(2)}) async-start(), calls=%async_computation.10 | async-start | bytes 786432 | tf_op jit(solution)/shard_map/reduce_scatter | solution.py:286
  4618.3 71.2 %reduce-scatter.11.cloned.1.call-start = ((), (), s32[]{:S(2)}) async-start(), calls=%async_computation.9 | async-start | bytes 1179648 | tf_op jit(solution)/shard_map/reduce_scatter | solution.py:285
  4626.0 63.5 %reduce-scatter.17.cloned.1.call-start = ((), (), s32[]{:S(2)}) async-start(), calls=%async_computation.12 | async-start | bytes 12582912 | tf_op jit(solution)/shard_map/reduce_scatter | solution.py:290
  4633.8 23.6 copy-start.3
  4633.9 25.1 copy-start.16
  4664.8 50.7 reduce-scatter.9.cloned.1.call-start
  4687.8 54.3 %reduce-scatter.19.cloned.1.call-start = ((), (), s32[]{:S(2)}) async-start(), calls=%async_computation.13 | async-start | bytes 1572864
  4689.4 428.7 %all-reduce.19.cloned.1.call-start = ((), (), s32[]{:S(2)}) async-start(), calls=%async_computation.14 | async-start | bytes 26607616 | tf_op jit(solution)/shard_map/psum | solution.py:292
  (48 other events, 351.8 us)
Sparse Core Ops, SparseCore 0:
  9.6 22.5 all-gather.3
  33.8 14.8 all-gather.5
  4616.0 8.6 reduce-scatter.14
  4626.8 9.0 reduce-scatter.12
  4638.7 9.3 reduce-scatter.10
  4664.9 17.9 reduce-scatter.16
  4688.0 27.4 reduce-scatter.8
  4717.7 9.7 reduce-scatter.18
  4735.1 383.0 all-reduce.18
where the time goes:
time: 5220 us; the launch traced here: 5140 us
  other arithmetic  3000 us (57%)
  local copies, waits for them, and re-layouts  1520 us (29%)
  waiting for transfers between devices  330 us (6%)
  blocking collectives  100 us (2%)
  loops' own time  84.7 us (2%)
  matrix products  83 us (2%)
    reduce_sum x352, other arithmetic, token_step(): return (carried, jnp.sum(step_c[:, :, None] * carried, axis=1))  849 us
    reduce_sum x616, other arithmetic, token_step(): (step_dt * step_u)[:, None, :] * step_b[:, :, None]  703 us
    while x1859, other arithmetic  643 us
    reduce_sum x88, other arithmetic, token_step(): step_dt[:, None, :] * decay_rate  615 us
    concatenate x528, local copies, waits for them, and re-layouts, span_run(): last_state, outputs = lax.scan(token_step, state_now, items, unroll=8)  454 us
    slice x616, local copies, waits for them, and re-layouts, span_run(): last_state, outputs = lax.scan(token_step, state_now, items, unroll=8)  394 us
    dynamic_update_slice x880, local copies, waits for them, and re-layouts, span_run(): last_state, outputs = lax.scan(token_step, state_now, items, unroll=8)  381 us
    psum x1, waiting for transfers between devices, shards(): lax.psum((grad_share[0], grad_share[1], grad_share[2], grad_share[3], gra...  293 us

commit v1 on v0

v1 whole, which is shorter than its diff:
```python
import functools
import math

import jax
import jax.numpy as jnp
from jax import lax
from jax.experimental import pallas as pl
from jax.experimental.pallas import tpu as pltpu
from jax.sharding import PartitionSpec as P

CHUNK = 64
WIDTH = 4
norm_eps = 1e-05

BIG = 1e30
LN2 = math.log(2.0)
LOG2E = 1.0 / LN2

def bcast(ref, row, lanes, width):
    return [ref[j, pl.ds(row, 8, stride=0), :] for j in range(width)]

def forward_kernel(dt_ref, u_ref, keep_ref, b_ref, c_ref, a_ref, y_ref, bound_ref, hs, dtm, dtu, ybuf, *, width):
    rows, inner = dt_ref.shape
    lanes_step = 128 * width
    @pl.when(pl.program_id(0) == 0)
    def _():
        hs[...] = jnp.zeros_like(hs)
    bound_ref[0] = hs[...]
    def chan(cb, _):
        base = pl.multiple_of(cb * lanes_step, lanes_step)
        for j in range(width):
            from_ = pl.ds(base + 128 * j, 128)
            d = dt_ref[:, from_]
            dtm[j] = jnp.where(keep_ref[...] > 0, d, BIG)
            dtu[j] = d * u_ref[:, from_]
        A = [[a_ref[pl.ds(8 * s, 8), pl.ds(base + 128 * j, 128)] for s in range(2)] for j in range(width)]
        def body(g, h):
            h = [list(p) for p in zip(h[:width], h[width:])]
            r0 = pl.multiple_of(g * 8, 8)
            for t in range(8):
                d = bcast(dtm, r0 + t, base, width)
                x = bcast(dtu, r0 + t, base, width)
                bt = [b_ref[pl.ds((r0 + t) * 16 + 8 * s, 8), :] for s in range(2)]
                ct = [c_ref[pl.ds((r0 + t) * 16 + 8 * s, 8), :] for s in range(2)]
                for j in range(width):
                    for s in range(2):
                        h[j][s] = jnp.exp2(d[j] * A[j][s]) * h[j][s] + x[j] * bt[s]
                    ybuf[j, pl.ds(t * 8, 8), :] = ct[0] * h[j][0] + ct[1] * h[j][1]
            for j in range(width):
                acc = ybuf[j, pl.ds(0, 8, stride=8), :]
                for s in range(1, 8):
                    acc = acc + ybuf[j, pl.ds(s, 8, stride=8), :]
                y_ref[pl.ds(r0, 8), pl.ds(base + 128 * j, 128)] = acc
            return tuple(p[0] for p in h) + tuple(p[1] for p in h)
        h0 = tuple(hs[pl.ds(8 * s, 8), pl.ds(base + 128 * j, 128)] for s in range(2) for j in range(width))
        h = lax.fori_loop(0, rows // 8, body, h0)
        for s in range(2):
            for j in range(width):
                hs[pl.ds(8 * s, 8), pl.ds(base + 128 * j, 128)] = h[s * width + j]
        return _
    lax.fori_loop(0, inner // lanes_step, chan, 0)

def scan_forward(dt, u, keep, b, c, a, chunk, width):
    T, DI = dt.shape
    n = T // chunk
    row = lambda w: pl.BlockSpec((chunk, w), lambda i: (i, 0))
    return pl.pallas_call(
        functools.partial(forward_kernel, width=width),
        grid=(n,),
        in_specs=[row(DI), row(DI), row(128), pl.BlockSpec((chunk * 16, 128), lambda i: (i, 0)), pl.BlockSpec((chunk * 16, 128), lambda i: (i, 0)),
                  pl.BlockSpec((16, DI), lambda i: (0, 0))],
        out_specs=[row(DI), pl.BlockSpec((1, 16, DI), lambda i: (i, 0, 0))],
        out_shape=[jax.ShapeDtypeStruct((T, DI), jnp.float32), jax.ShapeDtypeStruct((n, 16, DI), jnp.float32)],
        scratch_shapes=[pltpu.VMEM((16, DI), jnp.float32), pltpu.VMEM((width, chunk, 128), jnp.float32), pltpu.VMEM((width, chunk, 128), jnp.float32),
                        pltpu.VMEM((width, 64, 128), jnp.float32)],
        compiler_params=pltpu.CompilerParams(dimension_semantics=("arbitrary",), vmem_limit_bytes=56 << 20),
        name="scan_forward",
    )(dt, u, keep, b, c, a)

def backward_kernel(dt_ref, u_ref, dy_ref, keep_ref, b_ref, c_ref, a_ref, bound_ref, dd_ref, di_ref, db_ref, dc_ref, ga_ref,
               ws, dtm, dtu, dyb, hbuf, sbuf, qbuf, *, width):
    rows, inner = dt_ref.shape
    lanes_step = 128 * width
    @pl.when(pl.program_id(0) == 0)
    def _():
        ws[...] = jnp.zeros_like(ws)
        ga_ref[...] = jnp.zeros_like(ga_ref)
    db_ref[...] = jnp.zeros_like(db_ref)
    dc_ref[...] = jnp.zeros_like(dc_ref)
    def chan(cb, _):
        base = pl.multiple_of(cb * lanes_step, lanes_step)
        for j in range(width):
            from_ = pl.ds(base + 128 * j, 128)
            d = dt_ref[:, from_]
            dtm[j] = jnp.where(keep_ref[...] > 0, d, BIG)
            dtu[j] = d * u_ref[:, from_]
            dyb[j] = dy_ref[:, from_]
        A = [[a_ref[pl.ds(8 * s, 8), pl.ds(base + 128 * j, 128)] for s in range(2)] for j in range(width)]
        def again(g, h):
            h = [list(p) for p in zip(h[:width], h[width:])]
            r0 = pl.multiple_of(g * 8, 8)
            for t in range(8):
                d = bcast(dtm, r0 + t, base, width)
                x = bcast(dtu, r0 + t, base, width)
                bt = [b_ref[pl.ds((r0 + t) * 16 + 8 * s, 8), :] for s in range(2)]
                for j in range(width):
                    for s in range(2):
                        hbuf[pl.ds((r0 + t) * 16 + 8 * s, 8), pl.ds(128 * j, 128)] = h[j][s]
                        h[j][s] = jnp.exp2(d[j] * A[j][s]) * h[j][s] + x[j] * bt[s]
            return tuple(p[0] for p in h) + tuple(p[1] for p in h)
        h0 = tuple(bound_ref[0, pl.ds(8 * s, 8), pl.ds(base + 128 * j, 128)] for s in range(2) for j in range(width))
        h = lax.fori_loop(0, rows // 8, again, h0)
        for s in range(2):
            for j in range(width):
                hbuf[pl.ds(rows * 16 + 8 * s, 8), pl.ds(128 * j, 128)] = h[s * width + j]
        def body(k, carry):
            g_ = rows // 8 - 1 - k
            r0 = pl.multiple_of(g_ * 8, 8)
            w = [[carry[s * width + j] for s in range(2)] for j in range(width)]
            ga = [[carry[2 * width + s * width + j] for s in range(2)] for j in range(width)]
            for t in range(7, -1, -1):
                d = bcast(dtm, r0 + t, base, width)
                x = bcast(dtu, r0 + t, base, width)
                v = bcast(dyb, r0 + t, base, width)
                bt = [b_ref[pl.ds((r0 + t) * 16 + 8 * s, 8), :] for s in range(2)]
                ct = [c_ref[pl.ds((r0 + t) * 16 + 8 * s, 8), :] for s in range(2)]
                db = [None, None]
                dc = [None, None]
                for j in range(width):
                    qs, ss = None, None
                    for s in range(2):
                        hn = hbuf[pl.ds((r0 + t + 1) * 16 + 8 * s, 8), pl.ds(128 * j, 128)]
                        hp = hbuf[pl.ds((r0 + t) * 16 + 8 * s, 8), pl.ds(128 * j, 128)]
                        g = ct[s] * v[j] + w[j][s]
                        w[j][s] = jnp.exp2(d[j] * A[j][s]) * g
                        q = w[j][s] * hp
                        ga[j][s] = ga[j][s] + q * d[j]
                        qa = q * A[j][s]
                        sb = g * bt[s]
                        qs = qa if qs is None else qs + qa
                        ss = sb if ss is None else ss + sb
                        gx = g * x[j]
                        vh = v[j] * hn
                        db[s] = gx if db[s] is None else db[s] + gx
                        dc[s] = vh if dc[s] is None else dc[s] + vh
                    qbuf[j, pl.ds(t * 8, 8), :] = qs
                    sbuf[j, pl.ds(t * 8, 8), :] = ss
                for s in range(2):
                    rr = pl.ds((r0 + t) * 16 + 8 * s, 8)
                    db_ref[rr, :] = db_ref[rr, :] + db[s]
                    dc_ref[rr, :] = dc_ref[rr, :] + dc[s]
            for j in range(width):
                here = pl.ds(base + 128 * j, 128)
                q8 = qbuf[j, pl.ds(0, 8, stride=8), :]
                s8 = sbuf[j, pl.ds(0, 8, stride=8), :]
                for s in range(1, 8):
                    q8 = q8 + qbuf[j, pl.ds(s, 8, stride=8), :]
                    s8 = s8 + sbuf[j, pl.ds(s, 8, stride=8), :]
                dd_ref[pl.ds(r0, 8), here] = LN2 * q8 + u_ref[pl.ds(r0, 8), here] * s8
                di_ref[pl.ds(r0, 8), here] = dt_ref[pl.ds(r0, 8), here] * s8
            return tuple(w[j][s] for s in range(2) for j in range(width)) + tuple(ga[j][s] for s in range(2) for j in range(width))
        c0 = tuple(r[pl.ds(8 * s, 8), pl.ds(base + 128 * j, 128)] for r in (ws, ga_ref) for s in range(2) for j in range(width))
        out = lax.fori_loop(0, rows // 8, body, c0)
        k = 0
        for r in (ws, ga_ref):
            for s in range(2):
                for j in range(width):
                    r[pl.ds(8 * s, 8), pl.ds(base + 128 * j, 128)] = out[k]
                    k += 1
        return _
    lax.fori_loop(0, inner // lanes_step, chan, 0)

def scan_backward(dt, u, dy, keep, b, c, a, bound, chunk, width):
    T, DI = dt.shape
    n = T // chunk
    rev = lambda i: (n - 1 - i, 0)
    row = lambda w: pl.BlockSpec((chunk, w), rev)
    tall = pl.BlockSpec((chunk * 16, 128), rev)
    f32 = jnp.float32
    return pl.pallas_call(
        functools.partial(backward_kernel, width=width),
        grid=(n,),
        in_specs=[row(DI), row(DI), row(DI), row(128), tall, tall, pl.BlockSpec((16, DI), lambda i: (0, 0)),
                  pl.BlockSpec((1, 16, DI), lambda i: (n - 1 - i, 0, 0))],
        out_specs=[row(DI), row(DI), tall, tall, pl.BlockSpec((16, DI), lambda i: (0, 0))],
        out_shape=[jax.ShapeDtypeStruct((T, DI), f32)] * 2 + [jax.ShapeDtypeStruct((T * 16, 128), f32)] * 2 + [jax.ShapeDtypeStruct((16, DI), f32)],
        scratch_shapes=[pltpu.VMEM((16, DI), f32), pltpu.VMEM((width, chunk, 128), f32), pltpu.VMEM((width, chunk, 128), f32), pltpu.VMEM((width, chunk, 128), f32),
                        pltpu.VMEM((chunk * 16 + 16, 128 * width), f32), pltpu.VMEM((width, 64, 128), f32), pltpu.VMEM((width, 64, 128), f32)],
        compiler_params=pltpu.CompilerParams(dimension_semantics=("arbitrary",), vmem_limit_bytes=56 << 20),
        name="scan_backward",
    )(dt, u, dy, keep, b, c, a, bound)


def cluster_offsets(lengths, total_len):
    count = lengths.shape[1]
    ahead = jnp.arange(count)[:, None] < jnp.arange(count)[None, :]
    start_points = jnp.sum(jnp.where(ahead[None], lengths[:, :, None], 0), axis=1, dtype=jnp.int32)
    end_points = start_points + lengths
    where_at = jnp.arange(total_len, dtype=jnp.int32)
    inside = (where_at[None, None, :] >= start_points[:, :, None]) & (
        where_at[None, None, :] < end_points[:, :, None]
    )
    first_spot = jnp.sum(jnp.where(inside, start_points[:, :, None], 0), axis=1, dtype=jnp.int32)
    return where_at[None, :] - first_spot


def rms_piece(inputs, gain_vec):
    mean_sq = jnp.mean(inputs * inputs, axis=-1, keepdims=True)
    return inputs * lax.rsqrt(mean_sq + norm_eps) * gain_vec


def conv_piece(upper_part, conv_taps, conv_shift, offsets):
    tap_count = conv_taps.shape[0]
    total_len = upper_part.shape[0]
    summed = conv_shift + conv_taps[tap_count - 1] * upper_part
    for lag_steps in range(1, tap_count):
        shifted = jnp.pad(upper_part, ((lag_steps, 0), (0, 0)))[:total_len]
        summed = summed + conv_taps[tap_count - 1 - lag_steps] * jnp.where(
            (offsets >= lag_steps)[:, None], shifted, 0.0
        )
    return summed * jax.nn.sigmoid(summed)


def gate_piece(y_full, gate_z):
    return y_full * gate_z * jax.nn.sigmoid(gate_z)


def dot32(left, right, contract):
    return lax.dot_general(left, right, (contract, ((), ())), preferred_element_type=jnp.float32)


def reduced(grad, dim):
    share = lax.psum_scatter(grad.astype(jnp.bfloat16), "fsdp", scatter_dimension=dim, tiled=True)
    return lax.psum(share, "dp").astype(jnp.float32)


def shards(
    hidden_in,
    cluster_lengths,
    norm_gain,
    in_proj,
    conv_weight,
    conv_bias,
    x_proj,
    dt_proj,
    dt_bias,
    a_log,
    skip_gain,
    out_proj,
    out_grad,
):
    f32, bf16 = jnp.float32, jnp.bfloat16
    w_in = lax.all_gather(in_proj, "fsdp", axis=0, tiled=True)
    w_out = lax.all_gather(out_proj, "fsdp", axis=0, tiled=True)
    w_x = lax.all_gather(x_proj, "fsdp", axis=0, tiled=True)
    w_gain = lax.all_gather(norm_gain, "fsdp", axis=0, tiled=True)
    taps = conv_weight.shape[0]
    rank_dim = dt_proj.shape[0]
    state_dim = a_log.shape[0]
    packed = jnp.concatenate(
        [dt_proj, a_log, conv_weight, conv_bias[None], dt_bias[None], skip_gain[None]], axis=0
    )
    packed = lax.all_gather(packed, "fsdp", axis=1, tiled=True)
    w_dt = packed[:rank_dim]
    w_alog = packed[rank_dim : rank_dim + state_dim].astype(f32)
    rest = packed[rank_dim + state_dim :].astype(f32)
    conv_taps, conv_shift, b_dt, w_skip = rest[:taps], rest[taps], rest[taps + 1], rest[taps + 2]

    contexts_here, total_len, model_dim = hidden_in.shape
    inner_dim = conv_taps.shape[1]
    rows = contexts_here * total_len
    offsets = cluster_offsets(cluster_lengths, total_len).reshape(rows)
    keep = jnp.broadcast_to(jnp.where(offsets > 0, 1.0, 0.0).astype(f32)[:, None], (rows, 128))
    inputs = hidden_in.reshape(rows, model_dim).astype(f32)
    grad_rows = out_grad.reshape(rows, model_dim)
    gain_full = w_gain.astype(f32)
    normed16 = rms_piece(inputs, gain_full).astype(bf16)
    both = dot32(normed16, w_in, ((1,), (0,)))
    upper_part = both[:, :inner_dim]
    gate_z = both[:, inner_dim:]
    inner_act = conv_piece(upper_part, conv_taps, conv_shift, offsets)
    inner16 = inner_act.astype(bf16)
    projected = dot32(inner16, w_x, ((1,), (0,)))
    rank16 = projected[:, :rank_dim].astype(bf16)
    b_in = projected[:, rank_dim : rank_dim + state_dim]
    c_out = projected[:, rank_dim + state_dim :]
    dt_pre = dot32(rank16, w_dt, ((1,), (0,))) + b_dt
    delta_t = jax.nn.softplus(dt_pre)
    decay_rate = -jnp.exp(w_alog)
    spread = lambda v: jnp.broadcast_to(v[:, :, None], (rows, state_dim, 128)).reshape(rows * state_dim, 128)
    b_wide, c_wide = spread(b_in), spread(c_out)
    rate2 = decay_rate * LOG2E
    scan_y, boundary = scan_forward(delta_t, inner_act, keep, b_wide, c_wide, rate2, CHUNK, WIDTH)
    d_gated = dot32(grad_rows, w_out, ((1,), (1,)))
    y_full = scan_y + w_skip * inner_act
    gated16 = gate_piece(y_full, gate_z).astype(bf16)
    layer_out = (inputs + dot32(gated16, w_out, ((1,), (0,)))).astype(bf16)
    g_w_out = dot32(gated16, grad_rows, ((0,), (0,)))
    _, gate_pull = jax.vjp(gate_piece, y_full, gate_z)
    d_y, d_gate_z = gate_pull(d_gated)
    gate16 = d_gate_z.astype(bf16)
    g_w_gate = dot32(normed16, gate16, ((0,), (0,)))
    g_skip = jnp.sum(d_y * inner_act, axis=0)
    d_delta, d_inner_scan, d_bin, d_cout, rate_sum = scan_backward(
        delta_t, inner_act, d_y, keep, b_wide, c_wide, rate2, boundary, CHUNK, WIDTH
    )
    d_bin = jnp.sum(d_bin.reshape(rows, state_dim, 128), axis=-1)
    d_cout = jnp.sum(d_cout.reshape(rows, state_dim, 128), axis=-1)
    g_alog = rate_sum * decay_rate
    dt16 = (d_delta * jax.nn.sigmoid(dt_pre)).astype(bf16)
    g_b_dt = jnp.sum(dt16.astype(f32), axis=0)
    g_w_dt = dot32(rank16, dt16, ((0,), (0,)))
    d_rank = dot32(dt16, w_dt, ((1,), (1,)))
    proj16 = jnp.concatenate([d_rank, d_bin, d_cout], axis=-1).astype(bf16)
    g_w_x = dot32(proj16, inner16, ((0,), (0,)))
    d_inner = dot32(proj16, w_x, ((1,), (1,))) + d_inner_scan + d_y * w_skip
    _, conv_pull = jax.vjp(
        lambda part_u, taps_in, shift_in: conv_piece(part_u, taps_in, shift_in, offsets),
        upper_part,
        conv_taps,
        conv_shift,
    )
    d_upper, g_conv, g_b_conv = conv_pull(d_inner)
    upper16 = d_upper.astype(bf16)
    g_w_upper = dot32(normed16, upper16, ((0,), (0,)))
    d_normed = dot32(upper16, w_in[:, :inner_dim], ((1,), (1,))) + dot32(
        gate16, w_in[:, inner_dim:], ((1,), (1,))
    )
    _, norm_pull = jax.vjp(rms_piece, inputs, gain_full)
    d_inputs, g_gain = norm_pull(d_normed)
    input_grad = grad_rows.astype(f32) + d_inputs

    parts = lax.axis_size("fsdp")
    gain_row = jnp.pad(
        g_gain.reshape(parts, model_dim // parts), ((0, 0), (0, (inner_dim - model_dim) // parts))
    ).reshape(1, inner_dim)
    small = jnp.concatenate(
        [g_w_x, g_w_dt, g_alog, g_conv, g_b_conv[None], g_b_dt[None], g_skip[None], gain_row], axis=0
    )
    t_out = reduced(g_w_out, 0)
    t_gate = reduced(g_w_gate, 0)
    t_upper = reduced(g_w_upper, 0)
    t_small = reduced(small, 1)
    t_in = jnp.concatenate([t_upper, t_gate], axis=1)
    columns = rank_dim + 2 * state_dim
    at = 0
    picked = []
    for size in (columns, rank_dim, state_dim, taps, 1, 1, 1, 1):
        picked.append(t_small[at : at + size])
        at += size
    t_x, t_dt, t_alog, t_conv, t_b_conv, t_b_dt, t_skip, t_gain = picked
    return (
        layer_out.reshape(hidden_in.shape),
        input_grad.reshape(hidden_in.shape),
        t_gain[0, : model_dim // parts],
        t_in,
        t_conv,
        t_b_conv[0],
        t_x.T,
        t_dt,
        t_b_dt[0],
        t_alog,
        t_skip[0],
        t_out,
    )


def solution(mesh):
    placed = (
        P(("dp", "fsdp"), None, None),
        P(("dp", "fsdp"), None),
        P("fsdp"),
        P("fsdp", None),
        P(None, "fsdp"),
        P("fsdp"),
        P("fsdp", None),
        P(None, "fsdp"),
        P("fsdp"),
        P(None, "fsdp"),
        P("fsdp"),
        P("fsdp", None),
        P(("dp", "fsdp"), None, None),
    )
    return jax.shard_map(
        shards,
        mesh=mesh,
        in_specs=placed,
        out_specs=(
            P(("dp", "fsdp"), None, None),
            P(("dp", "fsdp"), None, None),
            P("fsdp"),
            P("fsdp", None),
            P(None, "fsdp"),
            P("fsdp"),
            P("fsdp", None),
            P(None, "fsdp"),
            P("fsdp"),
            P(None, "fsdp"),
            P("fsdp"),
            P("fsdp", None),
        ),
        check_vma=False,
    )
```

time: 5220 us -> 619 us (0.12); the launches traced: 5140 us -> 609 us
  other arithmetic: 3000 us -> 33.5 us
  local copies, waits for them, and re-layouts: 1520 us -> 34.8 us
  Pallas kernels: 0 us -> 130 us
  blocking collectives: 100 us -> 6.06 us
  loops' own time: 84.7 us -> 0 us
  waiting for transfers between devices: 330 us -> 273 us
    reduce_sum x1058 -> x4, other arithmetic: 2200 us -> 10.7 us  [the longest x1 3.54 us: shards(): d_cout = jnp.sum(d_cout.reshape(rows, state_dim, 128), axis=-1)]
    while x1859 -> x0, other arithmetic: 643 us -> none
    concatenate x528 -> x2, local copies, waits for them, and re-layouts: 454 us -> 3.47 us  [the longest x1 3.42 us: shards(): jnp.concatenate([g_w_x, g_w_dt, g_alog, g_conv, g_b_conv[None], g_b_dt[No...]
    dynamic_update_slice x957 -> x0, local copies, waits for them, and re-layouts: 431 us -> none  [the longest x880 381 us: span_run(): last_state, outputs = lax.scan(token_step, state_now, items, unroll=8)]
    slice x619 -> x10, local copies, waits for them, and re-layouts: 397 us -> 10.5 us  [the longest x4 5.78 us: shards(): picked.append(t_small[at:at + size])]
    pallas_call x0 -> x2, Pallas kernels: none -> 130 us  [the longest x1 94.9 us: scan_backward(): pl.pallas_call(functools.partial(backward_kernel, width=width), grid=(n,)...]
    concatenate x265 -> x1, other arithmetic: 134 us -> 4.48 us  [shards(): t_in = jnp.concatenate([t_upper, t_gate], axis=1)]
    dynamic_slice x396 -> x0, local copies, waits for them, and re-layouts: 108 us -> none  [the longest x110 92.2 us: take_block(): return lax.dynamic_slice_in_dim(array_in, begin_at, SPAN, 1)]
where the time goes in v1:
time: 619 us; the launch traced here: 609 us
  waiting for transfers between devices  273 us (44%)
  Pallas kernels  130 us (21%)
  matrix products  116 us (19%)
  local copies, waits for them, and re-layouts  34.8 us (6%)
  other arithmetic  33.5 us (5%)
  between operations  15.1 us (2%)
    psum x1, waiting for transfers between devices, reduced(): return lax.psum(share, 'dp').astype(jnp.float32)  221 us
    dot_general x14, matrix products, dot32(): lax.dot_general(left, right, (contract, ((), ())), preferred_element_type...  116 us
    pallas_call x1, Pallas kernels, scan_backward(): pl.pallas_call(functools.partial(backward_kernel, width=width), grid=(n,)...  94.9 us
    reduce_scatter x4, waiting for transfers between devices, reduced(): lax.psum_scatter(grad.astype(jnp.bfloat16), 'fsdp', scatter_dimension=dim...  35.6 us
    pallas_call x1, Pallas kernels, scan_forward(): pl.pallas_call(functools.partial(forward_kernel, width=width), grid=(n,),...  35.1 us
    all_gather x1, waiting for transfers between devices, shards(): w_in = lax.all_gather(in_proj, 'fsdp', axis=0, tiled=True)  15.3 us
  transfers between devices with their start and end apart: 7, of which 5 were waited for; matrix products, arithmetic and copies ran while one was open for 7% of the time, Pallas kernels for 0%

profile of v1, /device:TPU:0, one launch (start us, length us, event | category | flops | bytes accessed | tf_op | source)
XLA Modules:
  0.0 609.0 jit_solution(1822482454238915314)
XLA Ops:
  16.9 15.3 %all-gather.4.cloned.1.call-done = bf16[1024,4096]{1,0:T(8,128)(2,1)} async-done(((bf16[512,4096]{1,0:T(8,128)(2,1)}), bf16[1024,4096]{1,0:T(8,128)(2,1)}) %all-gather.4.cloned.1.call-update) | async-done | bytes 8388624 | tf_op jit(solution)/shard_map/all_gather | solution.py:253
  32.2 8.7 %fusion.50 = f32[704,4096]{1,0:T(8,128)S(1)} fusion(bf16[1024,4096]{1,0:T(8,128)(2,1)} %all-gather.4.cloned.1.call-done, bf16[1,704,1024]{2,1,0:T(8,128)(2,1)S(1)} %copy-done.1, f32[1024]{0:T(1024)S(1)} %bitcast.72, f32[704]{0:T(1024)S(1)} %fusion.41), kind=kOutput, calls=%fused_computation.102 | convolution fusion | flops 5908463616 | bytes 21371648 | tf_op jit(solution)/shard_map/dot_general | solution.py:229
  41.0 5.6 copy-done.4
  49.5 24.2 %multiply_reduce_fusion = (bf16[2048]{0:T(1024)(128)(2,1)S(1)}, f32[704,2048]{1,0:T(8,128)}, f32[704,2048]{1,0:T(8,128)S(1)}, f32[704,2048]{1,0:T(8,128)}, f32[704,2048]{1,0:T(8,128)}) fusion(f32[704,4096]{1,0:T(8,128)} %copy-done.4, f32[704,2048]{1,0:T(8,128)} %slice.133, pred[704]{0:T(1024)(128)(4,1)S(1)} %get-tuple-element.67, f32[2048]{0:T(1024)S(1)} %bitcast.78, ...), kind=kOutput, calls=%fused_computation.26 | convolution fusion | flops 2984507392 | bytes 40286272 | tf_op jit(solution)/shard_map/dot_general | solution.py:229
  74.6 7.6 %compare_select_fusion = (f32[704,2048]{1,0:T(8,128)}, f32[704,2048]{1,0:T(8,128)}) fusion(f32[2048]{0:T(1024)S(1)} %bitcast.69, bf16[87,2048]{1,0:T(8,128)(2,1)S(1)} %all_gather.15, f32[704,96]{0,1:T(8,128)S(1)} %fusion.34), kind=kOutput, calls=%fused_computation | convolution fusion | flops 194641920 | bytes 11902976 | tf_op jit(solution)/shard_map/dot_general | solution.py:229
  83.7 5.9 broadcast_in_dim.156.b_ref
  89.7 6.1 broadcast_in_dim.158.c_ref
  95.8 35.1 %scan_forward.1 = (f32[704,2048]{1,0:T(8,128)}, f32[11,16,2048]{2,1,0:T(8,128)}) custom-call(f32[704,2048]{1,0:T(8,128)} %get-tuple-element.69.dt_ref, f32[704,2048]{1,0:T(8,128)} %copy-done, f32[704,128]{1,0:T(8,128)} %broadcast_in_dim.154.keep_ref, f32[11264,128]{1,0:T(8,128)} %broadcast_in_dim.156.b_ref, f32[11264,128]{1,0:T(8,128)} %broadcast_in_dim.158.c_ref, ...), custom_call_target="tpu_custom_call" | custom-call | tf_op jit(solution)/shard_map/scan_forward/pallas_call | solution.py:67
  130.8 94.9 %scan_backward.1 = (f32[704,2048]{1,0:T(8,128)}, f32[704,2048]{1,0:T(8,128)}, f32[11264,128]{1,0:T(8,128)}, f32[11264,128]{1,0:T(8,128)}, f32[16,2048]{1,0:T(8,128)}) custom-call(f32[704,2048]{1,0:T(8,128)} %get-tuple-element.69.dt_ref, f32[704,2048]{1,0:T(8,128)} %copy-done, f32[704,2048]{1,0:T(8,128)} %get-tuple-element.41.dy_ref, ...), custom_call_target="tpu_custom_call" | custom-call | tf_op jit(solution)/shard_map/scan_backward/pallas_call | solution.py:180
  241.8 30.2 %fusion.52 = (bf16[2048]{0:T(1024)(128)(2,1)S(1)}, f32[2048]{0:T(1024)S(1)}, f32[2048]{0:T(1024)S(1)}, f32[2048]{0:T(1024)S(1)}, f32[2048]{0:T(1024)S(1)}, /*ind...) fusion(f32[704,4096]{1,0:T(8,128)} %copy-done.4, ...), kind=kOutput, calls=%fused_computation.103 | convolution fusion | flops 343541760 | bytes 81340480 | tf_op jit(solution)/shard_map/dot_general | solution.py:229
  272.1 7.6 %fusion.6 = bf16[704,2048]{1,0:T(8,128)(2,1)S(1)} fusion(f32[704,2048]{1,0:T(8,128)} %get-tuple-element.52, f32[704,2048]{1,0:T(8,128)} %get-tuple-element.51, f32[704,2048]{1,0:T(8,128)S(1)} %get-tuple-element.50, f32[704,2048]{1,0:T(8,128)} %get-tuple-element.71, f32[2048]{0:T(1024)S(1)} %bitcast.68), kind=kLoop, calls=%fused_computation.20 | loop fusion | flops 7208960 | bytes 25960448 | tf_op jit(solution)/shard_map/convert_element_type | solution.py:324
  279.8 6.4 %fusion.13 = f32[704,1024]{1,0:T(8,128)S(1)} fusion(bf16[704,2048]{1,0:T(8,128)(2,1)S(1)} %copy-done.23, bf16[1024,4096]{1,0:T(8,128)(2,1)} %all-gather.4.cloned.1.call-done), kind=kOutput, calls=%fused_computation.44 | convolution fusion | flops 2952790016 | bytes 9961472 | tf_op jit(solution)/shard_map/dot_general | solution.py:229
  286.2 7.4 %fusion.20 = (bf16[1024]{0:T(1024)(128)(2,1)S(1)}, f32[704]{0:T(1024)S(1)}, f32[704,1024]{1,0:T(8,128)}) fusion(bf16[1,704,1024]{2,1,0:T(8,128)(2,1)S(1)} %copy-done.2, f32[704]{0:T(1024)S(1)} %fusion.41, f32[1024]{0:T(1024)S(1)} %bitcast.73, f32[704,1024]{1,0:T(8,128)S(1)} %fusion.13, bf16[704,2048]{1,0:T(8,128)(2,1)S(1)} %fusion.6, ...), kind=kOutput, calls=%fused_computation.55 | convolution fusion | flops 2958555392 | bytes 14298624 | tf_op jit(solution)/shard_map/dot_general | solution.py:229
  297.2 7.1 %convolution_convert_fusion.1 = bf16[1024,2048]{1,0:T(8,128)(2,1)} fusion(bf16[704,2048]{1,0:T(8,128)(2,1)} %get-tuple-element.49, bf16[1,704,1024]{2,1,0:T(8,128)(2,1)S(1)} %copy-done.2, f32[1024]{0:T(1024)S(1)} %bitcast.74, f32[704]{0:T(1024)S(1)} %fusion.41), kind=kOutput, calls=%fused_computation.50 | convolution fusion | flops 2957770752 | bytes 8526592 | tf_op jit(solution)/shard_map/dot_general | solution.py:229
  304.4 7.2 %convolution_convert_fusion.2 = bf16[1024,2048]{1,0:T(8,128)(2,1)} fusion(bf16[704,2048]{1,0:T(8,128)(2,1)} %copy-done.3, bf16[1,704,1024]{2,1,0:T(8,128)(2,1)S(1)} %copy-done.2, f32[1024]{0:T(1024)S(1)} %bitcast.75, f32[704]{0:T(1024)S(1)} %fusion.41), kind=kOutput, calls=%fused_computation.51 | convolution fusion | flops 2957770752 | bytes 8526592 | tf_op jit(solution)/shard_map/dot_general | solution.py:229
  311.7 7.0 %convolution_convert_fusion = bf16[2048,1024]{1,0:T(8,128)(2,1)} fusion(bf16[704,2048]{1,0:T(8,128)(2,1)} %get-tuple-element.48, bf16[1,704,1024]{2,1,0:T(8,128)(2,1)S(1)} %copy-done.7), kind=kOutput, calls=%fused_computation.49 | convolution fusion | flops 2954887168 | bytes 8519680 | tf_op jit(solution)/shard_map/dot_general | solution.py:229
  318.8 3.9 reduce-scatter.9.cloned.1.call-done
  322.7 16.2 %reduce-scatter.7.cloned.1.call-done = bf16[512,2048]{1,0:T(8,128)(2,1)} async-done(((bf16[1024,2048]{1,0:T(8,128)(2,1)}), bf16[512,2048]{1,0:T(8,128)(2,1)}) %reduce-scatter.7.cloned.1.call-update) | async-done | bytes 2097168 | tf_op jit(solution)/shard_map/reduce_scatter | solution.py:233
  338.9 15.5 %reduce-scatter.11.cloned.1.call-done = bf16[1024,1024]{1,0:T(8,128)(2,1)} async-done(((bf16[2048,1024]{1,0:T(8,128)(2,1)}), bf16[1024,1024]{1,0:T(8,128)(2,1)}) %reduce-scatter.11.cloned.1.call-update) | async-done | bytes 2097168 | tf_op jit(solution)/shard_map/reduce_scatter | solution.py:233
  354.5 4.3 fusion.22
  358.8 4.5 fusion.29
  363.3 220.9 %all-reduce.14.cloned.1.call-done = (bf16[184,1024]{1,0:T(8,128)(2,1)}, bf16[512,2048]{1,0:T(8,128)(2,1)}, bf16[512,2048]{1,0:T(8,128)(2,1)}, bf16[1024,1024]{1,0:T(8,128)(2,1)}) async-done(((bf16[184,1024]{1,0:T(8,128)(2,1)}, bf16[512,2048]{1,0:T(8,128)(2,1)}, bf16[512,2048]{1,0:T(8,128)(2,1)}, bf16[1024,1024]{1,0:T(8,128)(2,1)}), (bf16[184,1024]{1,0:T(8,128)(2,1)}, bf16[512,2048]{1,0:T(8,128)(2,1)}, ...) | async-done | bytes 6668304 | tf_op jit(solution)/shard_map/psum | solution.py:234
  593.2 4.1 convert_element_type.94
  597.3 4.5 maximum_convert_fusion
  (124 shorter events, 43.8 us)
Async XLA Ops:
  7.3 5.7 copy-start.10
  7.3 7.8 %copy-start.22 = (s32[1,8]{1,0:T(1,128)S(1)}, s32[1,8]{1,0:T(1,128)}, u32[]{:S(2)}) copy-start(s32[1,8]{1,0:T(1,128)} %param.14) | copy-start | bytes 100
  7.3 8.0 %copy-start.1 = (bf16[1,704,1024]{2,1,0:T(8,128)(2,1)S(1)}, bf16[1,704,1024]{2,1,0:T(8,128)(2,1)}, u32[]{:S(2)}) copy-start(bf16[1,704,1024]{2,1,0:T(8,128)(2,1)} %param.13) | copy-start | bytes 4325380
  7.3 25.0 %all-gather.4.cloned.1.call-start = ((), (), s32[]{:S(2)}) async-start(), calls=%async_computation.4 | async-start | bytes 12582912 | tf_op jit(solution)/shard_map/all_gather | solution.py:253
  8.0 41.4 %all-gather.6.cloned.1.call-start = ((), (), s32[]{:S(2)}) async-start(), calls=%async_computation.5 | async-start | bytes 6291456 | tf_op jit(solution)/shard_map/all_gather | solution.py:254
  8.8 310.0 %reduce-scatter.5.cloned.1.call-start = ((), (), s32[]{:S(2)}) async-start(), calls=%async_computation.6 | async-start | bytes 1130496 | tf_op jit(solution)/shard_map/reduce_scatter | solution.py:233
  40.9 5.6 copy-start.4
  73.6 8.6 %copy-start = (f32[704,2048]{1,0:T(8,128)}, f32[704,2048]{1,0:T(8,128)S(1)}, u32[]{:S(2)}) copy-start(f32[704,2048]{1,0:T(8,128)S(1)} %get-tuple-element.42.u_ref) | copy-start | bytes 17301508
  74.6 7.6 %copy-start.8 = (f32[704,96]{0,1:T(8,128)}, f32[704,96]{0,1:T(8,128)S(1)}, u32[]{:S(2)}) copy-start(f32[704,96]{0,1:T(8,128)S(1)} %fusion.34) | copy-start | bytes 811012
  95.8 130.0 %slice-start = ((s8[5767168]{0:T(1024)(128)(4,1)}), s8[4194304]{0:T(1024)(128)(4,1)S(1)}, s32[]{:S(2)}) async-start(s8[5767168]{0:T(1024)(128)(4,1)} %bitcast.65), calls=%async_computation.11 | async-start | bytes 8388608
  130.8 94.9 %slice-start.1 = ((s8[5767168]{0:T(1024)(128)(4,1)}), s8[1572864]{0:T(1024)(128)(4,1)S(1)}, s32[]{:S(2)}) async-start(s8[5767168]{0:T(1024)(128)(4,1)} %bitcast.65), calls=%async_computation.12 | async-start | bytes 3145728
  225.7 4.5 copy-start.9
  230.9 7.6 %copy-start.11 = (f32[16,2048]{1,0:T(8,128)S(1)}, f32[16,2048]{1,0:T(8,128)}, u32[]{:S(2)}) copy-start(f32[16,2048]{1,0:T(8,128)} %get-tuple-element.25) | copy-start | bytes 393220
  272.1 7.7 %copy-start.23 = (bf16[704,2048]{1,0:T(8,128)(2,1)S(1)}, bf16[704,2048]{1,0:T(8,128)(2,1)}, u32[]{:S(2)}) copy-start(bf16[704,2048]{1,0:T(8,128)(2,1)} %get-tuple-element.49) | copy-start | bytes 8650756
  279.8 6.4 %copy-start.3 = (bf16[704,2048]{1,0:T(8,128)(2,1)}, bf16[704,2048]{1,0:T(8,128)(2,1)S(1)}, u32[]{:S(2)}) copy-start(bf16[704,2048]{1,0:T(8,128)(2,1)S(1)} %fusion.6) | copy-start | bytes 8650756
  279.8 6.4 %copy-start.2 = (bf16[1,704,1024]{2,1,0:T(8,128)(2,1)S(1)}, bf16[1,704,1024]{2,1,0:T(8,128)(2,1)}, u32[]{:S(2)}) copy-start(bf16[1,704,1024]{2,1,0:T(8,128)(2,1)} %param.13) | copy-start | bytes 4325380
  297.1 25.5 %reduce-scatter.9.cloned.1.call-start = ((), (), s32[]{:S(2)}) async-start(), calls=%async_computation.8 | async-start | bytes 6291456 | tf_op jit(solution)/shard_map/reduce_scatter | solution.py:233
  304.3 7.4 %copy-start.7 = (bf16[1,704,1024]{2,1,0:T(8,128)(2,1)S(1)}, bf16[1,704,1024]{2,1,0:T(8,128)(2,1)}, u32[]{:S(2)}) copy-start(bf16[1,704,1024]{2,1,0:T(8,128)(2,1)} %param.25) | copy-start | bytes 4325380
  304.3 34.5 %reduce-scatter.7.cloned.1.call-start = ((), (), s32[]{:S(2)}) async-start(), calls=%async_computation.7 | async-start | bytes 6291456 | tf_op jit(solution)/shard_map/reduce_scatter | solution.py:233
  311.6 42.8 %reduce-scatter.11.cloned.1.call-start = ((), (), s32[]{:S(2)}) async-start(), calls=%async_computation.9 | async-start | bytes 6291456 | tf_op jit(solution)/shard_map/reduce_scatter | solution.py:233
  318.7 35.8 %copy-start.14 = (f32[704]{0:T(1024)S(1)}, f32[704]{0:T(1024)}, u32[]{:S(2)}) copy-start(f32[704]{0:T(1024)} %copy-done.13) | copy-start | bytes 8452
  318.7 265.4 %all-reduce.14.cloned.1.call-start = ((), (), s32[]{:S(2)}) async-start(), calls=%async_computation.10 | async-start | bytes 13336576 | tf_op jit(solution)/shard_map/psum | solution.py:234
  584.1 13.1 %copy-start.5 = (bf16[512,2048]{1,0:T(8,128)(2,1)S(1)}, bf16[512,2048]{1,0:T(8,128)(2,1)}, u32[]{:S(2)}) copy-start(bf16[512,2048]{1,0:T(8,128)(2,1)} %get-tuple-element.37) | copy-start | bytes 6291460
  584.1 13.1 %copy-start.6 = (bf16[512,2048]{1,0:T(8,128)(2,1)S(1)}, bf16[512,2048]{1,0:T(8,128)(2,1)}, u32[]{:S(2)}) copy-start(bf16[512,2048]{1,0:T(8,128)(2,1)} %get-tuple-element.38) | copy-start | bytes 6291460
  (10 other events, 23.2 us)
Sparse Core Ops, SparseCore 0:
  9.7 22.5 all-gather.3
  33.8 14.8 all-gather.5
  297.3 9.4 reduce-scatter.4
  309.4 13.2 reduce-scatter.8
  325.5 13.3 reduce-scatter.6
  341.0 13.3 reduce-scatter.10
  362.0 222.1 all-reduce.13
